TPU v7x, 32 devices: a whole 2x2x4 slice. The times are simulated.
32 devices in a mesh: branch: 2 (over core), seq: 4 (over z), head: 4 (over y, x).
Axes of the slice: x: 2, y: 2, z: 4, core: 2. Of those that a mesh axis runs over, the one named last changes fastest.
Arguments:
- tokens: bfloat16 [1024, 3072], P('seq', 'head'), may hold values from -10 to 10
- valid_counts: int32 [4], P('seq'), may hold values from 1 to 256, 768 in all
- shared_qkv: bfloat16 [3072, 3, 1536], P('branch', None, 'head'), may hold values from -0.08479832 to 0.08479832
- shared_out: bfloat16 [1536, 3072], P('head', 'branch'), may hold values from -0.15625 to 0.15625
- skipped_qkv: bfloat16 [3072, 3, 1536], P('branch', None, 'head'), may hold values from -0.08479832 to 0.08479832
- skipped_out: bfloat16 [1536, 3072], P('head', 'branch'), may hold values from -0.15625 to 0.15625
- modulation: float32 [2, 3, 3072], replicated, may hold values from -3 to 3
- qk_gains: float32 [2, 2, 128], replicated, may hold values from 1.2 to 5.5
Outputs:
- branches: bfloat16 [2, 1024, 3072], P('branch', 'seq', 'head')
Inputs may be any that keep to these rules, and one draw needn't show every extreme that they name: `valid_counts`: each entry counts the leading real tokens of one shard of 256 slots; the rest are padding. The entries sum to 768 and one of them equals 256.
All inputs are finite; a program needn't handle non-finite values.
Results may differ from a plain program's by a relative error of at most 0.01.
Values may be sent and summed in bfloat16 or wider, within the bound.
No kernel may reach another device: no remote copies, remote signals or barrier semaphores. Data moves between devices by JAX's collectives and lax.ppermute only.
A program may use at most 128 MiB of HBM per device.

v0:
```python
import jax
import jax.numpy as jnp
from jax import lax
from jax.sharding import PartitionSpec as P

HEAD_DIM = 128


def modulate(x_rows, mod):
    whole = lax.all_gather(x_rows, "head", axis=1, tiled=True)
    xf = whole.astype(jnp.float32)
    mean = jnp.mean(xf, axis=1, keepdims=True)
    centered = xf - mean
    var = jnp.mean(centered * centered, axis=1, keepdims=True)
    normed = centered * lax.rsqrt(var + 1e-06)
    return (normed * (1.0 + mod[1]) + mod[0]).astype(jnp.bfloat16)


def attend_block(x_full, keep_full, qkv_weight, out_weight, mod, gains):
    rows, quarter = x_full.shape
    width = qkv_weight.shape[2]
    group = width // HEAD_DIM
    moded = modulate(x_full, mod)
    qkv = jnp.einsum(
        "rd,dsc->rsc",
        moded,
        lax.all_gather(qkv_weight, "branch", axis=0, tiled=True),
        preferred_element_type=jnp.float32,
    )
    qpart = qkv[:, 0].reshape(rows, group, HEAD_DIM)
    kpart = qkv[:, 1].reshape(rows, group, HEAD_DIM)
    query = (
        qpart * lax.rsqrt(jnp.mean(qpart * qpart, axis=2, keepdims=True) + 1e-06) * gains[0]
    ).astype(jnp.bfloat16)
    key = (
        kpart * lax.rsqrt(jnp.mean(kpart * kpart, axis=2, keepdims=True) + 1e-06) * gains[1]
    ).astype(jnp.bfloat16)
    key = key.reshape(rows, width)
    value = qkv[:, 2].astype(jnp.bfloat16)
    scale = 1.0 / HEAD_DIM**0.5
    keep_wire = keep_full.astype(jnp.bfloat16)
    peak = jnp.full((group, rows), -1e30, jnp.float32)
    key_piece = lax.all_gather(key, "seq", axis=0, tiled=True)
    value_piece = lax.all_gather(value, "seq", axis=0, tiled=True)
    keep_piece = lax.all_gather(keep_wire, "seq", axis=0, tiled=True)
    length = key_piece.shape[0]
    key_heads = key_piece.reshape(length, group, HEAD_DIM)
    value_heads = value_piece.reshape(length, group, HEAD_DIM)
    scores = (
        jnp.einsum("rhd,nhd->hrn", query, key_heads, preferred_element_type=jnp.float32) * scale
    )
    valid = keep_piece[None, None, :] > 0.5
    scores = jnp.where(valid, scores, -1e30)
    new_peak = jnp.maximum(peak, jnp.max(scores, axis=2))
    weights = jnp.where(valid, jnp.exp(scores - new_peak[:, :, None]), 0.0)
    total = jnp.sum(weights, axis=2)
    mixed = jnp.einsum(
        "hrn,nhd->hrd",
        weights.astype(jnp.bfloat16),
        value_heads,
        preferred_element_type=jnp.float32,
    )
    attended = (mixed / total[:, :, None]).astype(jnp.bfloat16)
    attended = attended.transpose(1, 0, 2).reshape(rows, width)
    projected = jnp.dot(
        attended,
        lax.all_gather(out_weight, "branch", axis=1, tiled=True),
        preferred_element_type=jnp.float32,
    )
    mine = lax.psum_scatter(projected, "head", scatter_dimension=1, tiled=True)
    gate = lax.dynamic_slice_in_dim(mod[2], lax.axis_index("head") * quarter, quarter, 0)
    return (x_full.astype(jnp.float32) + gate[None, :] * mine).astype(jnp.bfloat16)


def full_block(x_full, keep_full, qkv_weight, out_weight, mod, gains):
    updated = attend_block(x_full, keep_full, qkv_weight, out_weight, mod, gains)
    return updated


def per_device(
    tokens, valid_counts, shared_qkv, shared_out, skipped_qkv, skipped_out, modulation, qk_gains
):
    rows = tokens.shape[0]
    positions = jnp.arange(rows, dtype=jnp.int32)
    keep_all = (positions < valid_counts[0]).astype(jnp.float32)
    forked = full_block(tokens, keep_all, shared_qkv, shared_out, modulation[0], qk_gains[0])
    strong = full_block(forked, keep_all, skipped_qkv, skipped_out, modulation[1], qk_gains[1])
    result = jnp.where(lax.axis_index("branch") == 0, strong, forked)
    return result[None]


def solution(mesh):
    in_specs = (
        P("seq", "head"),
        P("seq"),
        P("branch", None, "head"),
        P("head", "branch"),
        P("branch", None, "head"),
        P("head", "branch"),
        P(),
        P(),
    )
    out_specs = P("branch", "seq", "head")
    return jax.shard_map(
        per_device, mesh=mesh, in_specs=in_specs, out_specs=out_specs, check_vma=False
    )
```

profile of v0, /device:TPU:0, one launch (start us, length us, event | category | flops | bytes accessed | tf_op | source)
XLA Modules:
  0.0 313.8 jit_solution(11347913517500845164)
XLA Ops:
  9.6 12.7 %all-gather.2 = bf16[4,1,256]{2,1,0:T(2,128)(2,1)S(1)} all-gather(bf16[1,1,256]{2,1,0:T(2,128)(2,1)S(1)} %reshape.146), channel_id=1, replica_groups=mesh['branch'=2,'seq'=4,'head'=4] {'seq'}, dimensions={0}, use_global_device_ids=true | all-gather | bytes 2560 | tf_op jit(solution)/shard_map/all_gather | solution.py:45
  22.3 20.5 %all-gather.10.cloned.1.call-done = bf16[256,3072]{1,0:T(8,128)(2,1)} async-done(((bf16[256,768]{1,0:T(8,128)(2,1)}), bf16[256,3072]{1,0:T(8,128)(2,1)}) %all-gather.10.cloned.1.call-update) | async-done | bytes 1572880 | tf_op jit(solution)/shard_map/all_gather | solution.py:10
  42.8 1.8 convert_reduce_fusion.1
  44.6 2.0 fusion.8
  46.6 15.7 %all-gather.12.cloned.1.call-done = bf16[3072,3,384]{2,0,1:T(8,128)(2,1)} async-done(((bf16[1536,3,384]{2,0,1:T(8,128)(2,1)}), bf16[3072,3,384]{2,0,1:T(8,128)(2,1)}) %all-gather.12.cloned.1.call-update) | async-done | bytes 7077904 | tf_op jit(solution)/shard_map/all_gather | solution.py:27
  62.3 5.3 %fusion.19 = f32[256,3,384]{2,0,1:T(8,128)S(1)} fusion(bf16[3072,3,384]{2,0,1:T(8,128)(2,1)} %all-gather.12.cloned.1.call-done, bf16[256,3072]{1,0:T(8,128)(2,1)S(1)} %copy-done, f32[3072]{0:T(1024)S(1)} %bitcast.90, f32[3072]{0:T(1024)S(1)} %bitcast.91, f32[256]{0:T(256)S(1)} %add_rsqrt_fusion.5, f32[256]{0:T(256)S(1)} %broadcast_multiply_fusion.1), kind=kOutput, calls=%fused_computation.27 | convolution fusion | flops 1816657920 | bytes 9857024 | tf_op jit(solution)/shard_map/rd,dsc->rsc/dot_general | solution.py:24
  68.1 19.8 %all_gather.37 = bf16[1024,384]{1,0:T(8,128)(2,1)S(1)} all-gather(bf16[256,384]{1,0:T(8,128)(2,1)S(1)} %fusion.61), channel_id=1, replica_groups=mesh['branch'=2,'seq'=4,'head'=4] {'seq'}, dimensions={0}, use_global_device_ids=true | all-gather | bytes 983040 | tf_op jit(solution)/shard_map/all_gather | solution.py:43
  88.4 18.0 %all-gather = bf16[1024,1,384]{2,0,1:T(8,128)(2,1)S(1)} all-gather(bf16[256,1,384]{2,0,1:T(8,128)(2,1)S(1)} %slice.109), channel_id=2, replica_groups=mesh['branch'=2,'seq'=4,'head'=4] {'seq'}, dimensions={0}, use_global_device_ids=true | all-gather | bytes 983040 | tf_op jit(solution)/shard_map/all_gather | solution.py:44
  108.5 0.9 fusion.53
  109.5 4.4 %fusion.78 = f32[256,3072]{1,0:T(8,128)} fusion(bf16[256,384]{0,1:T(8,128)(2,1)S(1)} %bitcast.87, bf16[384,3072]{1,0:T(8,128)(2,1)} %all-gather.14.cloned.1.call-done), kind=kOutput, calls=%fused_computation.104 | convolution fusion | flops 603979776 | bytes 5701632 | tf_op jit(solution)/shard_map/dot_general | solution.py:65
  114.0 43.3 %reduce-scatter.3.cloned.1.call-done = f32[256,768]{1,0:T(8,128)} async-done(((f32[256,3072]{1,0:T(8,128)}), f32[256,768]{1,0:T(8,128)}) %reduce-scatter.3.cloned.1.call-update) | async-done | bytes 786448 | tf_op jit(solution)/shard_map/reduce_scatter | solution.py:70
  157.3 2.0 add_convert_fusion.1
  160.7 29.6 %all-gather.16.cloned.1.call-done = bf16[256,3072]{1,0:T(8,128)(2,1)} async-done(((bf16[256,768]{1,0:T(8,128)(2,1)}), bf16[256,3072]{1,0:T(8,128)(2,1)}) %all-gather.16.cloned.1.call-update) | async-done | bytes 1572880 | tf_op jit(solution)/shard_map/all_gather | solution.py:10
  190.3 1.8 convert_reduce_fusion
  192.2 2.0 fusion.4
  194.1 15.5 %all-gather.18.cloned.1.call-done = bf16[3072,3,384]{2,0,1:T(8,128)(2,1)} async-done(((bf16[1536,3,384]{2,0,1:T(8,128)(2,1)}), bf16[3072,3,384]{2,0,1:T(8,128)(2,1)}) %all-gather.18.cloned.1.call-update) | async-done | bytes 7077904 | tf_op jit(solution)/shard_map/all_gather | solution.py:27
  209.7 5.3 %fusion.22 = f32[256,3,384]{2,0,1:T(8,128)S(1)} fusion(bf16[3072,3,384]{2,0,1:T(8,128)(2,1)} %all-gather.18.cloned.1.call-done, bf16[256,3072]{1,0:T(8,128)(2,1)S(1)} %copy-done.1, f32[3072]{0:T(1024)S(1)} %bitcast.88, f32[3072]{0:T(1024)S(1)} %bitcast.89, f32[256]{0:T(256)S(1)} %add_rsqrt_fusion.4, f32[256]{0:T(256)S(1)} %broadcast_multiply_fusion), kind=kOutput, calls=%fused_computation.29 | convolution fusion | flops 1816657920 | bytes 9857024 | tf_op jit(solution)/shard_map/rd,dsc->rsc/dot_general | solution.py:24
  215.5 19.8 %all_gather.42 = bf16[1024,384]{1,0:T(8,128)(2,1)S(1)} all-gather(bf16[256,384]{1,0:T(8,128)(2,1)S(1)} %fusion.59), channel_id=1, replica_groups=mesh['branch'=2,'seq'=4,'head'=4] {'seq'}, dimensions={0}, use_global_device_ids=true | all-gather | bytes 983040 | tf_op jit(solution)/shard_map/all_gather | solution.py:43
  235.8 18.2 %all-gather.1 = bf16[1024,1,384]{2,0,1:T(8,128)(2,1)S(1)} all-gather(bf16[256,1,384]{2,0,1:T(8,128)(2,1)S(1)} %slice.108), channel_id=3, replica_groups=mesh['branch'=2,'seq'=4,'head'=4] {'seq'}, dimensions={0}, use_global_device_ids=true | all-gather | bytes 983040 | tf_op jit(solution)/shard_map/all_gather | solution.py:44
  255.2 0.9 fusion.16
  256.1 0.9 fusion.47
  257.1 4.4 %fusion.79 = f32[256,3072]{1,0:T(8,128)} fusion(bf16[256,384]{0,1:T(8,128)(2,1)S(1)} %bitcast.86, bf16[384,3072]{1,0:T(8,128)(2,1)} %all-gather.20.cloned.1.call-done), kind=kOutput, calls=%fused_computation.105 | convolution fusion | flops 603979776 | bytes 5701632 | tf_op jit(solution)/shard_map/dot_general | solution.py:65
  261.5 43.4 %reduce-scatter.5.cloned.1.call-done = f32[256,768]{1,0:T(8,128)} async-done(((f32[256,3072]{1,0:T(8,128)}), f32[256,768]{1,0:T(8,128)}) %reduce-scatter.5.cloned.1.call-update) | async-done | bytes 786448 | tf_op jit(solution)/shard_map/reduce_scatter | solution.py:70
  304.9 2.0 fusion.57
  (75 shorter events, 9.1 us)
Async XLA Ops:
  6.5 2.3 copy-start.4
  6.5 2.3 copy-start.5
  6.5 36.2 %all-gather.10.cloned.1.call-start = ((), (), s32[]{:S(2)}) async-start(), calls=%async_computation.2 | async-start | bytes 1966080 | tf_op jit(solution)/shard_map/all_gather | solution.py:10
  7.3 55.0 %all-gather.12.cloned.1.call-start = ((), (), s32[]{:S(2)}) async-start(), calls=%async_computation.3 | async-start | bytes 10616832 | tf_op jit(solution)/shard_map/all_gather | solution.py:27
  8.0 101.5 %all-gather.14.cloned.1.call-start = ((), (), s32[]{:S(2)}) async-start(), calls=%async_computation.4 | async-start | bytes 3538944 | tf_op jit(solution)/shard_map/all_gather | solution.py:67
  8.7 148.6 %reduce-scatter.3.cloned.1.call-start = ((), (), s32[]{:S(2)}) async-start(), calls=%async_computation.5 | async-start | bytes 3932160 | tf_op jit(solution)/shard_map/reduce_scatter | solution.py:70
  42.8 19.5 %copy-start = (bf16[256,3072]{1,0:T(8,128)(2,1)S(1)}, bf16[256,3072]{1,0:T(8,128)(2,1)}, u32[]{:S(2)}) copy-start(bf16[256,3072]{1,0:T(8,128)(2,1)} %all-gather.10.cloned.1.call-done) | copy-start | bytes 4718596
  109.5 47.8 %copy-start.3 = (bf16[256,768]{1,0:T(8,128)(2,1)S(1)}, bf16[256,768]{1,0:T(8,128)(2,1)}, u32[]{:S(2)}) copy-start(bf16[256,768]{1,0:T(8,128)(2,1)} %param.8) | copy-start | bytes 1179652
  113.9 76.4 %all-gather.16.cloned.1.call-start = ((), (), s32[]{:S(2)}) async-start(), calls=%async_computation.6 | async-start | bytes 1966080 | tf_op jit(solution)/shard_map/all_gather | solution.py:10
  159.3 50.4 %all-gather.18.cloned.1.call-start = ((), (), s32[]{:S(2)}) async-start(), calls=%async_computation.7 | async-start | bytes 10616832 | tf_op jit(solution)/shard_map/all_gather | solution.py:27
  159.9 97.1 %all-gather.20.cloned.1.call-start = ((), (), s32[]{:S(2)}) async-start(), calls=%async_computation.8 | async-start | bytes 3538944 | tf_op jit(solution)/shard_map/all_gather | solution.py:67
  160.6 144.3 %reduce-scatter.5.cloned.1.call-start = ((), (), s32[]{:S(2)}) async-start(), calls=%async_computation.9 | async-start | bytes 3932160 | tf_op jit(solution)/shard_map/reduce_scatter | solution.py:70
  190.3 19.3 %copy-start.1 = (bf16[256,3072]{1,0:T(8,128)(2,1)S(1)}, bf16[256,3072]{1,0:T(8,128)(2,1)}, u32[]{:S(2)}) copy-start(bf16[256,3072]{1,0:T(8,128)(2,1)} %all-gather.16.cloned.1.call-done) | copy-start | bytes 4718596
  257.0 47.9 %copy-start.2 = (bf16[256,768]{1,0:T(8,128)(2,1)S(1)}, bf16[256,768]{1,0:T(8,128)(2,1)}, u32[]{:S(2)}) copy-start(bf16[256,768]{1,0:T(8,128)(2,1)} %add_convert_fusion.1) | copy-start | bytes 1179652
Sparse Core Ops, SparseCore 0:
  9.2 33.5 all-gather.9
  44.3 17.9 all-gather.11
  63.8 12.1 all-gather.13
  114.0 43.2 reduce-scatter.2
  159.4 30.8 all-gather.15
  191.7 17.9 all-gather.17
  211.2 12.1 all-gather.19
  261.6 43.2 reduce-scatter.4
where the time goes:
time: 314 us
  waiting for transfers between devices  172 us (55%)
  blocking collectives  88.5 us (28%)
  matrix products  22.8 us (7%)
  between operations  14.5 us (5%)
  other arithmetic  13.9 us (4%)
    reduce_scatter x2, waiting for transfers between devices, attend_block(): mine = lax.psum_scatter(projected, 'head', scatter_dimension=1, tiled=True)  86.7 us
    all_gather x2, waiting for transfers between devices, modulate(): whole = lax.all_gather(x_rows, 'head', axis=1, tiled=True)  50.1 us
    all_gather x2, blocking collectives, attend_block(): key_piece = lax.all_gather(key, 'seq', axis=0, tiled=True)  39.7 us
    all_gather x2, blocking collectives, attend_block(): value_piece = lax.all_gather(value, 'seq', axis=0, tiled=True)  36.2 us
    all_gather x2, waiting for transfers between devices, attend_block(): lax.all_gather(qkv_weight, 'branch', axis=0, tiled=True)  31.2 us
    all_gather x1, blocking collectives, attend_block(): keep_piece = lax.all_gather(keep_wire, 'seq', axis=0, tiled=True)  12.7 us
    dot_general x2, matrix products, attend_block(): jnp.einsum('rd,dsc->rsc', moded, lax.all_gather(qkv_weight, 'branch', axi...  10.5 us
    dot_general x2, matrix products, attend_block(): jnp.dot(attended, lax.all_gather(out_weight, 'branch', axis=1, tiled=True...  8.77 us
  transfers between devices with their start and end apart: 8, of which 6 were waited for; matrix products, arithmetic and copies ran while one was open for 8% of the time, Pallas kernels for 0%

commit v1 on v0

--- a/solution.py
+++ b/solution.py
@@ -40,8 +40,11 @@
     scale = 1.0 / HEAD_DIM**0.5
     keep_wire = keep_full.astype(jnp.bfloat16)
     peak = jnp.full((group, rows), -1e30, jnp.float32)
-    key_piece = lax.all_gather(key, "seq", axis=0, tiled=True)
-    value_piece = lax.all_gather(value, "seq", axis=0, tiled=True)
+    key_piece, value_piece = jnp.split(
+        lax.all_gather(jnp.concatenate([key, value], axis=1), "seq", axis=0, tiled=True),
+        [key.shape[1]],
+        axis=1,
+    )
     keep_piece = lax.all_gather(keep_wire, "seq", axis=0, tiled=True)
     length = key_piece.shape[0]
     key_heads = key_piece.reshape(length, group, HEAD_DIM)

time: 314 us -> 336 us (1.070)
  waiting for transfers between devices: 172 us -> 266 us
  blocking collectives: 88.5 us -> 11.2 us
    all_gather x4 -> x0, blocking collectives: 75.8 us -> none  [the longest x2 39.7 us: attend_block(): key_piece = lax.all_gather(key, 'seq', axis=0, tiled=True)]
    all_gather x0 -> x2, waiting for transfers between devices: none -> 62.8 us  [attend_block(): lax.all_gather(jnp.concatenate([key, value], axis=1), 'seq', axis=0, tile...]
    all_gather x2, waiting for transfers between devices: 50.1 us -> 64.8 us  [modulate(): whole = lax.all_gather(x_rows, 'head', axis=1, tiled=True)]
    all_gather x2, waiting for transfers between devices: 0.04 us -> 13.1 us  [attend_block(): lax.all_gather(out_weight, 'branch', axis=1, tiled=True)]
    split x0 -> x6, local copies, waits for them, and re-layouts: none -> 4.21 us  [attend_block(): jnp.split(lax.all_gather(jnp.concatenate([key, value], axis=1), 'seq', ax...]
    reduce_scatter x2, waiting for transfers between devices: 86.7 us -> 90.4 us  [attend_block(): mine = lax.psum_scatter(projected, 'head', scatter_dimension=1, tiled=True)]
  transfers between devices with their start and end apart: 8 -> 10, of which waited for: 6 -> 10; matrix products, arithmetic and copies ran while one was open for 8% -> 5% of each run, Pallas kernels for 0% -> 0%
where the time goes in v1:
time: 336 us
  waiting for transfers between devices  266 us (79%)
  matrix products  22.8 us (7%)
  other arithmetic  15.4 us (5%)
  between operations  14.5 us (4%)
  blocking collectives  11.2 us (3%)
  local copies, waits for them, and re-layouts  5.38 us (2%)
    reduce_scatter x2, waiting for transfers between devices, attend_block(): mine = lax.psum_scatter(projected, 'head', scatter_dimension=1, tiled=True)  90.4 us
    all_gather x2, waiting for transfers between devices, modulate(): whole = lax.all_gather(x_rows, 'head', axis=1, tiled=True)  64.8 us
    all_gather x2, waiting for transfers between devices, attend_block(): lax.all_gather(jnp.concatenate([key, value], axis=1), 'seq', axis=0, tile...  62.8 us
    all_gather x2, waiting for transfers between devices, attend_block(): lax.all_gather(qkv_weight, 'branch', axis=0, tiled=True)  31.4 us
    all_gather x2, waiting for transfers between devices, attend_block(): lax.all_gather(out_weight, 'branch', axis=1, tiled=True)  13.1 us
    all_gather x1, blocking collectives, attend_block(): keep_piece = lax.all_gather(keep_wire, 'seq', axis=0, tiled=True)  11.2 us
    dot_general x2, matrix products, attend_block(): jnp.einsum('rd,dsc->rsc', moded, lax.all_gather(qkv_weight, 'branch', axi...  10.5 us
    dot_general x2, matrix products, attend_block(): jnp.dot(attended, lax.all_gather(out_weight, 'branch', axis=1, tiled=True...  8.77 us
  transfers between devices with their start and end apart: 10, of which 10 were waited for; matrix products, arithmetic and copies ran while one was open for 5% of the time, Pallas kernels for 0%

profile of v1, /device:TPU:0, one launch (start us, length us, event | category | flops | bytes accessed | tf_op | source)
XLA Modules:
  0.0 335.6 jit_solution(936577158325862372)
XLA Ops:
  8.2 34.6 %all-gather.10.cloned.1.call-done = bf16[256,3072]{1,0:T(8,128)(2,1)} async-done(((bf16[256,768]{1,0:T(8,128)(2,1)}), bf16[256,3072]{1,0:T(8,128)(2,1)}) %all-gather.10.cloned.1.call-update) | async-done | bytes 1572880 | tf_op jit(solution)/shard_map/all_gather | solution.py:10
  42.8 1.8 convert_reduce_fusion.1
  44.6 2.0 fusion.8
  46.6 15.7 %all-gather.12.cloned.1.call-done = bf16[3072,3,384]{2,0,1:T(8,128)(2,1)} async-done(((bf16[1536,3,384]{2,0,1:T(8,128)(2,1)}), bf16[3072,3,384]{2,0,1:T(8,128)(2,1)}) %all-gather.12.cloned.1.call-update) | async-done | bytes 7077904 | tf_op jit(solution)/shard_map/all_gather | solution.py:27
  62.3 5.3 %fusion.19 = f32[256,3,384]{2,0,1:T(8,128)S(1)} fusion(bf16[3072,3,384]{2,0,1:T(8,128)(2,1)} %all-gather.12.cloned.1.call-done, bf16[256,3072]{1,0:T(8,128)(2,1)S(1)} %copy-done, f32[3072]{0:T(1024)S(1)} %bitcast.94, f32[3072]{0:T(1024)S(1)} %bitcast.95, f32[256]{0:T(256)S(1)} %add_rsqrt_fusion.5, f32[256]{0:T(256)S(1)} %broadcast_multiply_fusion.1), kind=kOutput, calls=%fused_computation.27 | convolution fusion | flops 1816657920 | bytes 9857024 | tf_op jit(solution)/shard_map/rd,dsc->rsc/dot_general | solution.py:24
  70.2 11.2 %all-gather = bf16[4,1,256]{2,1,0:T(2,128)(2,1)S(1)} all-gather(bf16[1,1,256]{2,1,0:T(2,128)(2,1)S(1)} %reshape.142), channel_id=1, replica_groups=mesh['branch'=2,'seq'=4,'head'=4] {'seq'}, dimensions={0}, use_global_device_ids=true | all-gather | bytes 2560 | tf_op jit(solution)/shard_map/all_gather | solution.py:48
  81.7 25.6 %all-gather.14.cloned.1.call-done = bf16[1024,768]{1,0:T(8,128)(2,1)} async-done(((bf16[256,768]{1,0:T(8,128)(2,1)}), bf16[1024,768]{1,0:T(8,128)(2,1)}) %all-gather.14.cloned.1.call-update) | async-done | bytes 1572880 | tf_op jit(solution)/shard_map/all_gather | solution.py:44
  107.3 1.5 fusion.78
  112.1 6.5 %all-gather.16.cloned.1.call-done = bf16[384,3072]{1,0:T(8,128)(2,1)} async-done(((bf16[384,1536]{1,0:T(8,128)(2,1)}), bf16[384,3072]{1,0:T(8,128)(2,1)}) %all-gather.16.cloned.1.call-update) | async-done | bytes 2359312 | tf_op jit(solution)/shard_map/all_gather | solution.py:70
  118.5 4.4 %fusion.82 = f32[256,3072]{1,0:T(8,128)} fusion(bf16[256,384]{0,1:T(8,128)(2,1)S(1)} %bitcast.91, bf16[384,3072]{1,0:T(8,128)(2,1)} %all-gather.16.cloned.1.call-done), kind=kOutput, calls=%fused_computation.110 | convolution fusion | flops 603979776 | bytes 5701632 | tf_op jit(solution)/shard_map/dot_general | solution.py:68
  123.0 45.2 %reduce-scatter.3.cloned.1.call-done = f32[256,768]{1,0:T(8,128)} async-done(((f32[256,3072]{1,0:T(8,128)}), f32[256,768]{1,0:T(8,128)}) %reduce-scatter.3.cloned.1.call-update) | async-done | bytes 786448 | tf_op jit(solution)/shard_map/reduce_scatter | solution.py:73
  168.2 2.0 add_convert_fusion.1
  171.0 30.2 %all-gather.18.cloned.1.call-done = bf16[256,3072]{1,0:T(8,128)(2,1)} async-done(((bf16[256,768]{1,0:T(8,128)(2,1)}), bf16[256,3072]{1,0:T(8,128)(2,1)}) %all-gather.18.cloned.1.call-update) | async-done | bytes 1572880 | tf_op jit(solution)/shard_map/all_gather | solution.py:10
  201.2 1.8 convert_reduce_fusion
  203.0 2.0 fusion.4
  205.0 15.7 %all-gather.20.cloned.1.call-done = bf16[3072,3,384]{2,0,1:T(8,128)(2,1)} async-done(((bf16[1536,3,384]{2,0,1:T(8,128)(2,1)}), bf16[3072,3,384]{2,0,1:T(8,128)(2,1)}) %all-gather.20.cloned.1.call-update) | async-done | bytes 7077904 | tf_op jit(solution)/shard_map/all_gather | solution.py:27
  220.7 5.3 %fusion.22 = f32[256,3,384]{2,0,1:T(8,128)S(1)} fusion(bf16[3072,3,384]{2,0,1:T(8,128)(2,1)} %all-gather.20.cloned.1.call-done, bf16[256,3072]{1,0:T(8,128)(2,1)S(1)} %copy-done.1, f32[3072]{0:T(1024)S(1)} %bitcast.92, f32[3072]{0:T(1024)S(1)} %bitcast.93, f32[256]{0:T(256)S(1)} %add_rsqrt_fusion.4, f32[256]{0:T(256)S(1)} %broadcast_multiply_fusion), kind=kOutput, calls=%fused_computation.29 | convolution fusion | flops 1816657920 | bytes 9857024 | tf_op jit(solution)/shard_map/rd,dsc->rsc/dot_general | solution.py:24
  228.5 37.2 %all-gather.22.cloned.1.call-done = bf16[1024,768]{1,0:T(8,128)(2,1)} async-done(((bf16[256,768]{1,0:T(8,128)(2,1)}), bf16[1024,768]{1,0:T(8,128)(2,1)}) %all-gather.22.cloned.1.call-update) | async-done | bytes 1572880 | tf_op jit(solution)/shard_map/all_gather | solution.py:44
  265.7 1.5 fusion.77
  269.5 0.9 fusion.47
  270.5 6.6 %all-gather.24.cloned.1.call-done = bf16[384,3072]{1,0:T(8,128)(2,1)} async-done(((bf16[384,1536]{1,0:T(8,128)(2,1)}), bf16[384,3072]{1,0:T(8,128)(2,1)}) %all-gather.24.cloned.1.call-update) | async-done | bytes 2359312 | tf_op jit(solution)/shard_map/all_gather | solution.py:70
  277.1 4.4 %fusion.83 = f32[256,3072]{1,0:T(8,128)} fusion(bf16[256,384]{0,1:T(8,128)(2,1)S(1)} %bitcast.90, bf16[384,3072]{1,0:T(8,128)(2,1)} %all-gather.24.cloned.1.call-done), kind=kOutput, calls=%fused_computation.111 | convolution fusion | flops 603979776 | bytes 5701632 | tf_op jit(solution)/shard_map/dot_general | solution.py:68
  281.5 45.2 %reduce-scatter.5.cloned.1.call-done = f32[256,768]{1,0:T(8,128)} async-done(((f32[256,3072]{1,0:T(8,128)}), f32[256,768]{1,0:T(8,128)}) %reduce-scatter.5.cloned.1.call-update) | async-done | bytes 786448 | tf_op jit(solution)/shard_map/reduce_scatter | solution.py:73
  326.7 2.0 fusion.57
  (81 shorter events, 12.7 us)
Async XLA Ops:
  6.5 1.5 copy-start.5
  6.5 1.6 copy-start.4
  6.5 36.2 %all-gather.10.cloned.1.call-start = ((), (), s32[]{:S(2)}) async-start(), calls=%async_computation.2 | async-start | bytes 1966080 | tf_op jit(solution)/shard_map/all_gather | solution.py:10
  7.3 55.0 %all-gather.12.cloned.1.call-start = ((), (), s32[]{:S(2)}) async-start(), calls=%async_computation.3 | async-start | bytes 10616832 | tf_op jit(solution)/shard_map/all_gather | solution.py:27
  8.0 99.3 %all-gather.14.cloned.1.call-start = ((), (), s32[]{:S(2)}) async-start(), calls=%async_computation.4 | async-start | bytes 1966080 | tf_op jit(solution)/shard_map/all_gather | solution.py:44
  42.8 19.5 %copy-start = (bf16[256,3072]{1,0:T(8,128)(2,1)S(1)}, bf16[256,3072]{1,0:T(8,128)(2,1)}, u32[]{:S(2)}) copy-start(bf16[256,3072]{1,0:T(8,128)(2,1)} %all-gather.10.cloned.1.call-done) | copy-start | bytes 4718596
  68.9 49.6 %all-gather.16.cloned.1.call-start = ((), (), s32[]{:S(2)}) async-start(), calls=%async_computation.5 | async-start | bytes 3538944 | tf_op jit(solution)/shard_map/all_gather | solution.py:70
  69.5 98.7 %reduce-scatter.3.cloned.1.call-start = ((), (), s32[]{:S(2)}) async-start(), calls=%async_computation.6 | async-start | bytes 3932160 | tf_op jit(solution)/shard_map/reduce_scatter | solution.py:73
  118.5 49.7 %copy-start.3 = (bf16[256,768]{1,0:T(8,128)(2,1)S(1)}, bf16[256,768]{1,0:T(8,128)(2,1)}, u32[]{:S(2)}) copy-start(bf16[256,768]{1,0:T(8,128)(2,1)} %param.8) | copy-start | bytes 1179652
  123.0 78.2 %all-gather.18.cloned.1.call-start = ((), (), s32[]{:S(2)}) async-start(), calls=%async_computation.7 | async-start | bytes 1966080 | tf_op jit(solution)/shard_map/all_gather | solution.py:10
  170.2 50.5 %all-gather.20.cloned.1.call-start = ((), (), s32[]{:S(2)}) async-start(), calls=%async_computation.8 | async-start | bytes 10616832 | tf_op jit(solution)/shard_map/all_gather | solution.py:27
  170.9 94.7 %all-gather.22.cloned.1.call-start = ((), (), s32[]{:S(2)}) async-start(), calls=%async_computation.9 | async-start | bytes 1966080 | tf_op jit(solution)/shard_map/all_gather | solution.py:44
  201.2 19.5 %copy-start.1 = (bf16[256,3072]{1,0:T(8,128)(2,1)S(1)}, bf16[256,3072]{1,0:T(8,128)(2,1)}, u32[]{:S(2)}) copy-start(bf16[256,3072]{1,0:T(8,128)(2,1)} %all-gather.18.cloned.1.call-done) | copy-start | bytes 4718596
  227.3 49.8 %all-gather.24.cloned.1.call-start = ((), (), s32[]{:S(2)}) async-start(), calls=%async_computation.10 | async-start | bytes 3538944 | tf_op jit(solution)/shard_map/all_gather | solution.py:70
  228.1 98.7 %reduce-scatter.5.cloned.1.call-start = ((), (), s32[]{:S(2)}) async-start(), calls=%async_computation.11 | async-start | bytes 3932160 | tf_op jit(solution)/shard_map/reduce_scatter | solution.py:73
  277.1 49.7 %copy-start.2 = (bf16[256,768]{1,0:T(8,128)(2,1)S(1)}, bf16[256,768]{1,0:T(8,128)(2,1)}, u32[]{:S(2)}) copy-start(bf16[256,768]{1,0:T(8,128)(2,1)} %add_convert_fusion.1) | copy-start | bytes 1179652
Sparse Core Ops, SparseCore 0:
  9.2 33.5 all-gather.9
  44.3 17.9 all-gather.11
  69.1 38.1 all-gather.13
  108.7 9.8 all-gather.15
  123.1 45.0 reduce-scatter.2
  170.3 30.8 all-gather.17
  202.7 17.9 all-gather.19
  227.4 38.1 all-gather.21
  267.2 9.8 all-gather.23
  281.6 45.0 reduce-scatter.4
